TPU v7x, 32 devices: a whole 2x2x4 slice. The times are simulated.
32 devices in a mesh: harm: 16 (over z, x, core), bus: 2 (over y).
Axes of the slice: x: 2, y: 2, z: 4, core: 2. Of those that a mesh axis runs over, the one named last changes fastest.
Arguments:
- conv_volt: bfloat16 [2, 64, 128, 128], P(None, None, ('bus', 'harm')), may hold values from -0.75 to 0.75
- conv_power: float32 [128, 128], P(('bus', 'harm')), may hold values from 0.2 to 2
- conv_type: int32 [128], P(('bus', 'harm')), may hold values from 0 to 7
- type_steep: float32 [8], replicated, may hold values from 0.5 to 4
- conv_bus: int32 [128], P(('bus', 'harm')), may hold values from 0 to 511, as said below
- admittance: float32 [2, 4, 64, 512], P(None, None, 'harm', 'bus'), may hold values from -0.5 to 1
- link_offset: int32 [3, 512], P(None, 'bus'), may hold values from -8 to 8, as said below
Outputs:
- bus_volt: bfloat16 [2, 64, 512, 128], P(None, 'harm', 'bus')
- conv_next: bfloat16 [2, 64, 128, 128], P(None, None, ('bus', 'harm'))
Inputs may be any that keep to these rules, and one draw needn't show every extreme that they name: `conv_bus`: converter c is attached to one of the buses from (c // 4) * 16 to (c // 4 + 1) * 16 - 1; a bus may carry several converters. `link_offset`: the first line of every bus spans exactly 8 buses, up or down; the others span 1 to 8 buses; no offset is zero.
All inputs are finite; a program needn't handle non-finite values.
Results may differ from a plain program's by a relative error of at most 0.0057.
Values may be sent and summed in bfloat16 or wider, within the bound.
A program may use at most 64 MiB of HBM per device.

v0:
```python
import math
import jax
import jax.numpy as jnp
from jax import lax
from jax.sharding import PartitionSpec as P

H = 64
NT = 1024
REACH = 8
ITERS = 3


def as_sent(array):
    return jax.tree.map(lambda a: a.astype(jnp.bfloat16) if a.dtype == jnp.float32 else a, array)


def extended_2(cells, sides, width):
    for axis, dim in sides:
        count = lax.axis_size(axis)
        ends = count - 1
        head = lax.slice_in_dim(cells, 0, width, axis=dim)
        tail = lax.slice_in_dim(cells, cells.shape[dim] - width, cells.shape[dim], axis=dim)
        cells = jnp.concatenate(
            [
                lax.ppermute(tail, axis, [(i, (i + 1) % count) for i in range(ends)]),
                cells,
                lax.ppermute(head, axis, [((i + 1) % count, i) for i in range(ends)]),
            ],
            axis=dim,
        )
    return cells


def make_basis():
    orders = jnp.arange(1, H + 1, dtype=jnp.int32)
    samples = jnp.arange(NT, dtype=jnp.int32)
    phases = (orders[:, None] * samples[None, :] % NT).astype(jnp.float32) * (2.0 * math.pi / NT)
    return jnp.concatenate([jnp.cos(phases), -jnp.sin(phases)], axis=0).astype(jnp.bfloat16)


def complex_product(left_real, left_imag, right_real, right_imag):
    return (
        left_real * right_real - left_imag * right_imag,
        left_real * right_imag + left_imag * right_real,
    )


def line_sum(inject_real, inject_imag, volt_real, volt_imag, lines_real, lines_imag, targets):
    total_real, total_imag = (inject_real, inject_imag)
    for line_num in range(targets.shape[0]):
        near_real = jnp.take(volt_real, targets[line_num], axis=1)
        near_imag = jnp.take(volt_imag, targets[line_num], axis=1)
        term_real, term_imag = complex_product(
            lines_real[line_num][:, :, None], lines_imag[line_num][:, :, None], near_real, near_imag
        )
        total_real = total_real + term_real
        total_imag = total_imag + term_imag
    return (total_real, total_imag)


def local(conv_volt, conv_power, conv_type, type_steep, conv_bus, admittance, link_offset):
    block_rows = admittance.shape[3]
    conv_count = conv_volt.shape[2]
    snapshots = conv_volt.shape[3]
    first_bus = lax.axis_index("bus") * block_rows
    harmonic_basis = make_basis()
    matches = conv_type[:, None] == jnp.arange(type_steep.shape[0], dtype=jnp.int32)[None, :]
    steepness = jnp.sum(jnp.where(matches, type_steep[None, :], 0.0), axis=1)
    volt_rows = conv_volt.reshape(2 * H, conv_count, snapshots)
    block_size = min(conv_count, 4)
    waveform = jnp.einsum(
        "kcs,kn->csn", volt_rows, harmonic_basis, preferred_element_type=jnp.float32
    )
    current = (
        conv_power[0:block_size, :, None] * jnp.tanh(steepness[0:block_size, None, None] * waveform)
    ).astype(jnp.bfloat16)
    spectra = jnp.einsum(
        "csn,kn->kcs", current, harmonic_basis, preferred_element_type=jnp.float32
    ) * NT ** (-0.5)
    pieces = spectra.astype(jnp.bfloat16)
    spectra = pieces.reshape(2, H, conv_count, snapshots)
    received = lax.all_to_all(spectra, "harm", split_axis=1, concat_axis=2, tiled=True)
    block_bus = lax.all_gather(conv_bus, "harm", axis=0, tiled=True) - first_bus
    summed = (
        jnp.zeros((2, received.shape[1], block_rows, snapshots), jnp.float32)
        .at[:, :, block_bus, :]
        .add(received.astype(jnp.float32))
    )
    injection = summed.astype(jnp.bfloat16)
    inject_real = injection[0].astype(jnp.float32)
    inject_imag = injection[1].astype(jnp.float32)
    inverse_real = admittance[0, 0][:, :, None]
    inverse_imag = admittance[1, 0][:, :, None]
    volt_real, volt_imag = complex_product(inverse_real, inverse_imag, inject_real, inject_imag)
    targets = jnp.arange(block_rows, dtype=jnp.int32)[None, :] + REACH + link_offset
    for sweep_index in range(ITERS - 1):
        extended = extended_2(as_sent(jnp.stack([volt_real, volt_imag])), (("bus", 2),), REACH)
        total_real, total_imag = line_sum(
            inject_real,
            inject_imag,
            extended[0],
            extended[1],
            admittance[0, 1:],
            admittance[1, 1:],
            targets,
        )
        volt_real, volt_imag = complex_product(inverse_real, inverse_imag, total_real, total_imag)
    bus_volt = jnp.stack([volt_real, volt_imag]).astype(jnp.bfloat16)
    picked = jnp.take(bus_volt, block_bus, axis=2)
    conv_next = lax.all_to_all(picked, "harm", split_axis=2, concat_axis=1, tiled=True)
    return (bus_volt, conv_next)


def solution(mesh):
    in_specs = (
        P(None, None, ("bus", "harm"), None),
        P(("bus", "harm"), None),
        P(("bus", "harm")),
        P(),
        P(("bus", "harm")),
        P(None, None, "harm", "bus"),
        P(None, "bus"),
    )
    out_specs = (P(None, "harm", "bus", None), P(None, None, ("bus", "harm"), None))
    return jax.shard_map(local, mesh=mesh, in_specs=in_specs, out_specs=out_specs, check_vma=False)
```

profile of v0, /device:TPU:0, one launch (start us, length us, event | category | flops | bytes accessed | tf_op | source)
XLA Modules:
  0.0 89.9 jit_solution(17024910230587955081)
XLA Ops:
  0.7 1.2 %cosine_convert_fusion = (bf16[64,1024]{1,0:T(8,128)(2,1)S(1)}, bf16[64,1024]{1,0:T(8,128)(2,1)S(1)}) fusion(s32[64]{0:T(128)S(1)} %iota_add_fusion.1), kind=kLoop, calls=%fused_computation.105 | loop fusion | flops 1114112 | bytes 262400 | tf_op jit(solution)/shard_map/convert.15
  2.8 1.3 %fusion.3 = bf16[128,4,128]{2,0,1:T(8,128)(2,1)S(1)} fusion(f32[4]{0:T(128)S(1)} %select_reduce_fusion, f32[4,128]{1,0:T(4,128)} %param.10, bf16[64,1024]{1,0:T(8,128)(2,1)S(1)} %get-tuple-element.41, bf16[64,1024]{1,0:T(8,128)(2,1)S(1)} %get-tuple-element.40, bf16[128,4,128]{2,1,0:T(4,128)(2,1)S(1)} %bitcast.148), kind=kOutput, calls=%fused_computation.18 | convolution fusion | flops 271187968 | bytes 526352 | tf_op jit(solution)/shard_map/csn,kn->kcs/dot_general | solution.py:77
  4.9 7.4 %all-to-all-start = ((bf16[2,64,4,128]{3,0,2,1:T(2,128)(2,1)}), bf16[2,64,4,128]{3,0,2,1:T(2,128)(2,1)S(1)}, u32[]{:S(2)}, u32[]{:S(2)}) async-start(bf16[2,64,4,128]{3,0,2,1:T(2,128)(2,1)} %copy.57), calls=%async_computation | async-start | bytes 262144 | tf_op jit(solution)/shard_map/all_to_all | solution.py:82
  13.9 12.4 %all-reduce = s32[64]{0:T(128)S(1)} all-reduce(s32[64]{0:T(128)S(1)} %dynamic-update-slice), channel_id=1, replica_groups=mesh['harm'=16,'bus'=2] {'harm'}, use_global_device_ids=true, to_apply=%add | all-reduce | flops 64 | bytes 512
  27.1 3.5 %scatter_fusion = f32[2,4,256,128]{3,1,2,0:T(4,128)S(1)} fusion(f32[2,4,256,128]{3,1,2,0:T(4,128)S(1)} %broadcast_in_dim.45, s32[64]{0:T(128)S(1)} %get-tuple-element.12, f32[64,2,4,128]{3,2,1,0:T(4,128)S(1)} %bitcast.149), kind=kCustom, calls=%fused_computation.13 | custom fusion | flops 65536 | bytes 786688 | tf_op jit(solution)/shard_map/scatter-add | solution.py:87
  31.5 3.4 %collective-permute-start = (bf16[2,4,8,128]{3,1,2,0:T(4,128)(2,1)S(1)}, bf16[2,4,8,128]{3,1,2,0:T(4,128)(2,1)S(1)}, u32[]{:S(2)}, u32[]{:S(2)}) collective-permute-start(bf16[2,4,8,128]{3,1,2,0:T(4,128)(2,1)S(1)} %get-tuple-element.27), channel_id=1, source_target_pairs={{0,1},{2,3},{4,5},{6,7},{8,9},{10,11},{12,13},{14,15},{16,17},{18,... | collective-permute-start | bytes 49160 | tf_op jit(solution)/shard_map/ppermute | solution.py:25
  35.0 1.3 %collective-permute-start.1 = (bf16[2,4,8,128]{3,1,2,0:T(4,128)(2,1)S(1)}, bf16[2,4,8,128]{3,1,2,0:T(4,128)(2,1)S(1)}, u32[]{:S(2)}, u32[]{:S(2)}) collective-permute-start(bf16[2,4,8,128]{3,1,2,0:T(4,128)(2,1)S(1)} %get-tuple-element.28), channel_id=1, source_target_pairs={{1,0},{3,2},{5,4},{7,6},{9,8},{11,10},{13,12},{15,14},{17,16},{19,... | collective-permute-start | bytes 49160 | tf_op jit(solution)/shard_map/ppermute | solution.py:27
  37.2 3.4 %collective-permute-done.1 = bf16[2,4,8,128]{3,1,2,0:T(4,128)(2,1)S(1)} collective-permute-done((bf16[2,4,8,128]{3,1,2,0:T(4,128)(2,1)S(1)}, bf16[2,4,8,128]{3,1,2,0:T(4,128)(2,1)S(1)}, u32[]{:S(2)}, u32[]{:S(2)}) %collective-permute-start.1) | collective-permute-done | bytes 16416 | tf_op jit(solution)/shard_map/ppermute | solution.py:27
  41.3 1.0 %gather_fusion.1 = bf16[256,4,128]{2,1,0:T(4,128)(2,1)S(1)} fusion(bf16[4,272,128]{2,0,1:T(4,128)(2,1)S(1)} %get-tuple-element.24, s32[1024]{0:T(1024)S(1)} %pad_clamp_fusion.3), kind=kCustom, calls=%fused_computation.clone | custom fusion | bytes 525312 | tf_op jit(solution)/shard_map/jit(_take)/gather | solution.py:51
  43.3 1.0 %gather_fusion.3 = bf16[256,4,128]{2,1,0:T(4,128)(2,1)S(1)} fusion(bf16[4,272,128]{2,0,1:T(4,128)(2,1)S(1)} %get-tuple-element.24, s32[1024]{0:T(1024)S(1)} %pad_clamp_fusion.2), kind=kCustom, calls=%fused_computation.2.clone | custom fusion | bytes 525312 | tf_op jit(solution)/shard_map/jit(_take)/gather | solution.py:51
  44.3 1.0 %gather_fusion.4 = bf16[256,4,128]{2,1,0:T(4,128)(2,1)S(1)} fusion(bf16[4,272,128]{2,0,1:T(4,128)(2,1)S(1)} %get-tuple-element.23, s32[1024]{0:T(1024)S(1)} %pad_clamp_fusion.2), kind=kCustom, calls=%fused_computation.3.clone | custom fusion | bytes 525312 | tf_op jit(solution)/shard_map/jit(_take)/gather | solution.py:52
  45.2 1.7 %gather_fusion.5 = bf16[256,4,128]{2,1,0:T(4,128)(2,1)} fusion(bf16[4,272,128]{2,0,1:T(4,128)(2,1)S(1)} %get-tuple-element.24, s32[1024]{0:T(1024)S(1)} %pad_clamp_fusion.1), kind=kCustom, calls=%fused_computation.4.clone | custom fusion | bytes 525312 | tf_op jit(solution)/shard_map/jit(_take)/gather | solution.py:51
  46.9 1.7 %gather_fusion.6 = bf16[256,4,128]{2,1,0:T(4,128)(2,1)} fusion(bf16[4,272,128]{2,0,1:T(4,128)(2,1)S(1)} %get-tuple-element.23, s32[1024]{0:T(1024)S(1)} %pad_clamp_fusion.1), kind=kCustom, calls=%fused_computation.5.clone | custom fusion | bytes 525312 | tf_op jit(solution)/shard_map/jit(_take)/gather | solution.py:52
  48.6 5.4 %fusion.37 = (bf16[1,4,256,128]{3,1,2,0:T(4,128)(2,1)S(1)}, f32[4,256,128]{2,0,1:T(4,128)S(1)}, f32[4,256,128]{2,0,1:T(4,128)S(1)}) fusion(f32[4,256]{0,1:T(8,128)S(1)} %copy.61, f32[4,256]{0,1:T(8,128)S(1)} %copy.53, bf16[256,4,128]{2,1,0:T(4,128)(2,1)} %gather_fusion.5, f32[4,256]{0,1:T(8,128)S(1)} %copy.66, bf16[256,4,128]{2,1,0:T(4,128)(2,1)} %gather_fusion.6, ...), kind=kLoop, calls=%fused_computation.96 | loop fusion | flops 5505024 | bytes 3441408 | tf_op jit(solution)/shard_map/stack | solution.py:97
  54.6 1.6 %collective-permute-start.2 = (bf16[2,4,8,128]{3,1,2,0:T(4,128)(2,1)S(1)}, bf16[2,4,8,128]{3,1,2,0:T(4,128)(2,1)S(1)}, u32[]{:S(2)}, u32[]{:S(2)}) collective-permute-start(bf16[2,4,8,128]{3,1,2,0:T(4,128)(2,1)S(1)} %get-tuple-element.25), channel_id=1, source_target_pairs={{0,1},{2,3},{4,5},{6,7},{8,9},{10,11},{12,13},{14,15},{16,17},{18,... | collective-permute-start | bytes 49160 | tf_op jit(solution)/shard_map/ppermute | solution.py:25
  56.3 1.5 %collective-permute-start.3 = (bf16[2,4,8,128]{3,1,2,0:T(4,128)(2,1)S(1)}, bf16[2,4,8,128]{3,1,2,0:T(4,128)(2,1)S(1)}, u32[]{:S(2)}, u32[]{:S(2)}) collective-permute-start(bf16[2,4,8,128]{3,1,2,0:T(4,128)(2,1)S(1)} %get-tuple-element.26), channel_id=1, source_target_pairs={{1,0},{3,2},{5,4},{7,6},{9,8},{11,10},{13,12},{15,14},{17,16},{19,... | collective-permute-start | bytes 49160 | tf_op jit(solution)/shard_map/ppermute | solution.py:27
  57.8 4.1 %collective-permute-done.3 = bf16[2,4,8,128]{3,1,2,0:T(4,128)(2,1)S(1)} collective-permute-done((bf16[2,4,8,128]{3,1,2,0:T(4,128)(2,1)S(1)}, bf16[2,4,8,128]{3,1,2,0:T(4,128)(2,1)S(1)}, u32[]{:S(2)}, u32[]{:S(2)}) %collective-permute-start.3) | collective-permute-done | bytes 16416 | tf_op jit(solution)/shard_map/ppermute | solution.py:27
  63.6 1.0 %gather_fusion.9 = bf16[256,4,128]{2,1,0:T(4,128)(2,1)S(1)} fusion(bf16[4,272,128]{2,0,1:T(4,128)(2,1)S(1)} %get-tuple-element.22, s32[1024]{0:T(1024)S(1)} %pad_clamp_fusion.2), kind=kCustom, calls=%fused_computation.8.clone | custom fusion | bytes 525312 | tf_op jit(solution)/shard_map/jit(_take)/gather | solution.py:51
  65.5 1.0 %gather_fusion.10 = bf16[256,4,128]{2,1,0:T(4,128)(2,1)S(1)} fusion(bf16[4,272,128]{2,0,1:T(4,128)(2,1)S(1)} %get-tuple-element.21, s32[1024]{0:T(1024)S(1)} %pad_clamp_fusion.2), kind=kCustom, calls=%fused_computation.9.clone | custom fusion | bytes 525312 | tf_op jit(solution)/shard_map/jit(_take)/gather | solution.py:52
  66.5 1.7 %gather_fusion.12 = bf16[256,4,128]{2,1,0:T(4,128)(2,1)} fusion(bf16[4,272,128]{2,0,1:T(4,128)(2,1)S(1)} %get-tuple-element.21, s32[1024]{0:T(1024)S(1)} %pad_clamp_fusion.1), kind=kCustom, calls=%fused_computation.11.clone | custom fusion | bytes 525312 | tf_op jit(solution)/shard_map/jit(_take)/gather | solution.py:52
  68.2 1.7 %gather_fusion.11 = bf16[256,4,128]{2,1,0:T(4,128)(2,1)} fusion(bf16[4,272,128]{2,0,1:T(4,128)(2,1)S(1)} %get-tuple-element.22, s32[1024]{0:T(1024)S(1)} %pad_clamp_fusion.1), kind=kCustom, calls=%fused_computation.10.clone | custom fusion | bytes 525312 | tf_op jit(solution)/shard_map/jit(_take)/gather | solution.py:51
  69.8 5.4 %fusion.39 = (bf16[1,4,256,128]{3,1,2,0:T(4,128)(2,1)S(1)}, f32[4,256,128]{2,0,1:T(4,128)S(1)}, f32[4,256,128]{2,0,1:T(4,128)S(1)}) fusion(f32[4,256]{0,1:T(8,128)S(1)} %copy.61, f32[4,256]{0,1:T(8,128)S(1)} %copy.53, bf16[256,4,128]{2,1,0:T(4,128)(2,1)} %gather_fusion.11, f32[4,256]{0,1:T(8,128)S(1)} %copy.66, bf16[256,4,128]{2,1,0:T(4,128)(2,1)} %gather_fusion.12, ...), kind=kLoop, calls=%fused_computation.98 | loop fusion | flops 5505024 | bytes 3441408 | tf_op jit(solution)/shard_map/stack | solution.py:108
  77.8 3.5 %all-to-all-start.1 = ((bf16[2,4,64,128]{3,1,0,2:T(4,128)(2,1)}), bf16[2,4,64,128]{3,1,0,2:T(4,128)(2,1)S(1)}, u32[]{:S(2)}, u32[]{:S(2)}) async-start(bf16[2,4,64,128]{3,1,0,2:T(4,128)(2,1)} %select_bitcast_fusion), calls=%async_computation.1 | async-start | bytes 262144 | tf_op jit(solution)/shard_map/all_to_all | solution.py:110
  82.2 7.0 %all-to-all-done.1 = bf16[2,4,64,128]{3,1,0,2:T(4,128)(2,1)S(1)} async-done(((bf16[2,4,64,128]{3,1,0,2:T(4,128)(2,1)}), bf16[2,4,64,128]{3,1,0,2:T(4,128)(2,1)S(1)}, u32[]{:S(2)}, u32[]{:S(2)}) %all-to-all-start.1) | async-done | bytes 131104 | tf_op jit(solution)/shard_map/all_to_all | solution.py:110
  (62 shorter events, 14.0 us)
Async XLA Ops:
  0.6 2.1 %copy-start = (bf16[2,64,4,128]{3,2,1,0:T(4,128)(2,1)S(1)}, bf16[2,64,4,128]{3,2,1,0:T(4,128)(2,1)}, u32[]{:S(2)}) copy-start(bf16[2,64,4,128]{3,2,1,0:T(4,128)(2,1)} %param.9) | copy-start | bytes 393220
  2.8 9.6 %copy-start.2 = (s32[3,256]{1,0:T(4,128)S(1)}, s32[3,256]{1,0:T(4,128)}, u32[]{:S(2)}) copy-start(s32[3,256]{1,0:T(4,128)} %param.15) | copy-start | bytes 9220
  2.8 9.6 %copy-start.1 = (f32[2,4,4,256]{3,2,1,0:T(4,128)S(1)}, f32[2,4,4,256]{3,2,1,0:T(4,128)}, u32[]{:S(2)}) copy-start(f32[2,4,4,256]{3,2,1,0:T(4,128)} %param.14) | copy-start | bytes 98308
  2.8 9.7 %copy-start.4 = (u32[32]{0:T(128)S(1)}, u32[32]{0:T(128)}, u32[]{:S(2)}) copy-start(u32[32]{0:T(128)} %constant.65) | copy-start | bytes 388
  2.8 10.9 %copy-start.3 = (s32[4]{0:T(128)S(1)}, s32[4]{0:T(128)}, u32[]{:S(2)}) copy-start(s32[4]{0:T(128)} %param.13) | copy-start | bytes 52
  4.9 21.8 %all-to-all-start = ((bf16[2,64,4,128]{3,0,2,1:T(2,128)(2,1)}), bf16[2,64,4,128]{3,0,2,1:T(2,128)(2,1)S(1)}, u32[]{:S(2)}, u32[]{:S(2)}) async-start(bf16[2,64,4,128]{3,0,2,1:T(2,128)(2,1)} %copy.57), calls=%async_computation | async-start | bytes 262144 | tf_op jit(solution)/shard_map/all_to_all | solution.py:82
  31.5 5.6 %collective-permute-start = (bf16[2,4,8,128]{3,1,2,0:T(4,128)(2,1)S(1)}, bf16[2,4,8,128]{3,1,2,0:T(4,128)(2,1)S(1)}, u32[]{:S(2)}, u32[]{:S(2)}) collective-permute-start(bf16[2,4,8,128]{3,1,2,0:T(4,128)(2,1)S(1)} %get-tuple-element.27), channel_id=1, source_target_pairs={{0,1},{2,3},{4,5},{6,7},{8,9},{10,11},{12,13},{14,15},{16,17},{18,... | collective-permute-start | bytes 49160 | tf_op jit(solution)/shard_map/ppermute | solution.py:25
  35.0 5.6 %collective-permute-start.1 = (bf16[2,4,8,128]{3,1,2,0:T(4,128)(2,1)S(1)}, bf16[2,4,8,128]{3,1,2,0:T(4,128)(2,1)S(1)}, u32[]{:S(2)}, u32[]{:S(2)}) collective-permute-start(bf16[2,4,8,128]{3,1,2,0:T(4,128)(2,1)S(1)} %get-tuple-element.28), channel_id=1, source_target_pairs={{1,0},{3,2},{5,4},{7,6},{9,8},{11,10},{13,12},{15,14},{17,16},{19,... | collective-permute-start | bytes 49160 | tf_op jit(solution)/shard_map/ppermute | solution.py:27
  54.6 3.1 %collective-permute-start.2 = (bf16[2,4,8,128]{3,1,2,0:T(4,128)(2,1)S(1)}, bf16[2,4,8,128]{3,1,2,0:T(4,128)(2,1)S(1)}, u32[]{:S(2)}, u32[]{:S(2)}) collective-permute-start(bf16[2,4,8,128]{3,1,2,0:T(4,128)(2,1)S(1)} %get-tuple-element.25), channel_id=1, source_target_pairs={{0,1},{2,3},{4,5},{6,7},{8,9},{10,11},{12,13},{14,15},{16,17},{18,... | collective-permute-start | bytes 49160 | tf_op jit(solution)/shard_map/ppermute | solution.py:25
  56.3 5.6 %collective-permute-start.3 = (bf16[2,4,8,128]{3,1,2,0:T(4,128)(2,1)S(1)}, bf16[2,4,8,128]{3,1,2,0:T(4,128)(2,1)S(1)}, u32[]{:S(2)}, u32[]{:S(2)}) collective-permute-start(bf16[2,4,8,128]{3,1,2,0:T(4,128)(2,1)S(1)} %get-tuple-element.26), channel_id=1, source_target_pairs={{1,0},{3,2},{5,4},{7,6},{9,8},{11,10},{13,12},{15,14},{17,16},{19,... | collective-permute-start | bytes 49160 | tf_op jit(solution)/shard_map/ppermute | solution.py:27
  77.8 11.4 %all-to-all-start.1 = ((bf16[2,4,64,128]{3,1,0,2:T(4,128)(2,1)}), bf16[2,4,64,128]{3,1,0,2:T(4,128)(2,1)S(1)}, u32[]{:S(2)}, u32[]{:S(2)}) async-start(bf16[2,4,64,128]{3,1,0,2:T(4,128)(2,1)} %select_bitcast_fusion), calls=%async_computation.1 | async-start | bytes 262144 | tf_op jit(solution)/shard_map/all_to_all | solution.py:110
where the time goes:
time: 91.1 us; the launch traced here: 89.9 us
  other arithmetic  20.9 us (23%)
  local copies, waits for them, and re-layouts  20.1 us (22%)
  starting transfers between devices  18.7 us (21%)
  waiting for transfers between devices  14.6 us (16%)
  blocking collectives  12.4 us (14%)
  between operations  1.79 us (2%)
  matrix products  1.34 us (1%)
    unnamed x1, blocking collectives  12.4 us
    ppermute x2, waiting for transfers between devices, extended_2(): lax.ppermute(head, axis, [((i + 1) % count, i) for i in range(ends)])  7.56 us
    all_to_all x1, starting transfers between devices, local(): lax.all_to_all(spectra, 'harm', split_axis=1, concat_axis=2, tiled=True)  7.38 us
    gather x6, local copies, waits for them, and re-layouts, line_sum(): near_real = jnp.take(volt_real, targets[line_num], axis=1)  7.25 us
    gather x6, local copies, waits for them, and re-layouts, line_sum(): near_imag = jnp.take(volt_imag, targets[line_num], axis=1)  7.24 us
    all_to_all x1, waiting for transfers between devices, local(): lax.all_to_all(picked, 'harm', split_axis=2, concat_axis=1, tiled=True)  7.01 us
    another operation x3, other arithmetic, local(): bus_volt = jnp.stack([volt_real, volt_imag]).astype(jnp.bfloat16)  6.37 us
    another operation x2, other arithmetic, local(): jnp.stack([volt_real, volt_imag])  6 us
  transfers between devices with their start and end apart: 6, of which 3 were waited for; matrix products, arithmetic and copies ran while one was open for 3% of the time, Pallas kernels for 0%

commit v1 on v0

--- a/solution.py
+++ b/solution.py
@@ -79,7 +79,10 @@
     ) * NT ** (-0.5)
     pieces = spectra.astype(jnp.bfloat16)
     spectra = pieces.reshape(2, H, conv_count, snapshots)
-    received = lax.all_to_all(spectra, "harm", split_axis=1, concat_axis=2, tiled=True)
+    received = jnp.concatenate(
+        lax.all_to_all(jnp.stack(jnp.split(spectra, lax.axis_size("harm"), axis=1)), "harm", 0, 0),
+        axis=2,
+    )
     block_bus = lax.all_gather(conv_bus, "harm", axis=0, tiled=True) - first_bus
     summed = (
         jnp.zeros((2, received.shape[1], block_rows, snapshots), jnp.float32)

time: 91.1 us -> 98.1 us (1.077)
  local copies, waits for them, and re-layouts: 20.1 us -> 27.2 us
    unnamed x14 -> x39, local copies, waits for them, and re-layouts: 1.73 us -> 10.8 us
    gather x6, local copies, waits for them, and re-layouts: 7.25 us -> 6.02 us  [line_sum(): near_real = jnp.take(volt_real, targets[line_num], axis=1)]
  transfers between devices with their start and end apart: 6 -> 6, of which waited for: 3 -> 3; matrix products, arithmetic and copies ran while one was open for 3% -> 4% of each run, Pallas kernels for 0% -> 0%
where the time goes in v1:
time: 98.1 us; the launch traced here: 97.2 us
  local copies, waits for them, and re-layouts  27.2 us (28%)
  other arithmetic  21 us (21%)
  starting transfers between devices  18.7 us (19%)
  waiting for transfers between devices  14.6 us (15%)
  blocking collectives  12.4 us (13%)
  between operations  1.85 us (2%)
  matrix products  1.47 us (1%)
    unnamed x1, blocking collectives  12.4 us
    unnamed x39, local copies, waits for them, and re-layouts  10.8 us
    ppermute x2, waiting for transfers between devices, extended_2(): lax.ppermute(head, axis, [((i + 1) % count, i) for i in range(ends)])  7.56 us
    all_to_all x1, starting transfers between devices, local(): lax.all_to_all(jnp.stack(jnp.split(spectra, lax.axis_size('harm'), axis=1...  7.38 us
    all_to_all x1, waiting for transfers between devices, local(): lax.all_to_all(picked, 'harm', split_axis=2, concat_axis=1, tiled=True)  7.01 us
    gather x6, local copies, waits for them, and re-layouts, line_sum(): near_imag = jnp.take(volt_imag, targets[line_num], axis=1)  6.57 us
    gather x6, local copies, waits for them, and re-layouts, line_sum(): near_real = jnp.take(volt_real, targets[line_num], axis=1)  6.02 us
    another operation x2, other arithmetic, local(): jnp.stack([volt_real, volt_imag])  5.95 us
  transfers between devices with their start and end apart: 6, of which 3 were waited for; matrix products, arithmetic and copies ran while one was open for 4% of the time, Pallas kernels for 0%

profile of v1, /device:TPU:0, one launch (start us, length us, event | category | flops | bytes accessed | tf_op | source)
XLA Modules:
  0.0 97.2 jit_solution(3293214078848983362)
XLA Ops:
  0.7 1.2 %cosine_convert_fusion = (bf16[64,1024]{1,0:T(8,128)(2,1)S(1)}, bf16[64,1024]{1,0:T(8,128)(2,1)S(1)}) fusion(s32[64]{0:T(128)S(1)} %iota_add_fusion.1), kind=kLoop, calls=%fused_computation.104 | loop fusion | flops 1114112 | bytes 262400 | tf_op jit(solution)/shard_map/convert.14
  2.8 1.5 %fusion.3 = bf16[128,4,128]{2,0,1:T(8,128)(2,1)S(1)} fusion(f32[4]{0:T(128)S(1)} %select_reduce_fusion, f32[4,128]{1,0:T(4,128)} %param.10, bf16[64,1024]{1,0:T(8,128)(2,1)S(1)} %get-tuple-element.37, bf16[64,1024]{1,0:T(8,128)(2,1)S(1)} %get-tuple-element.36, bf16[128,4,128]{2,1,0:T(4,128)(2,1)S(1)} %bitcast.209), kind=kOutput, calls=%fused_computation.18 | convolution fusion | flops 271187968 | bytes 526352 | tf_op jit(solution)/shard_map/csn,kn->kcs/dot_general | solution.py:77
  14.0 7.4 %all-to-all-start = ((bf16[16,2,4,4,128]{4,2,1,3,0:T(4,128)(2,1)}), bf16[16,2,4,4,128]{4,2,1,3,0:T(4,128)(2,1)S(1)}, u32[]{:S(2)}, u32[]{:S(2)}) async-start(bf16[16,2,4,4,128]{4,2,1,3,0:T(4,128)(2,1)} %constant_dynamic-update-slice_fusion), calls=%async_computation | async-start | bytes 262144 | tf_op jit(solution)/shard_map/all_to_all | solution.py:83
  23.0 12.4 %all-reduce = s32[64]{0:T(128)S(1)} all-reduce(s32[64]{0:T(128)S(1)} %dynamic-update-slice), channel_id=1, replica_groups=mesh['harm'=16,'bus'=2] {'harm'}, use_global_device_ids=true, to_apply=%add | all-reduce | flops 64 | bytes 512
  37.0 3.5 %scatter_fusion = f32[2,4,256,128]{3,1,2,0:T(4,128)S(1)} fusion(f32[2,4,256,128]{3,1,2,0:T(4,128)S(1)} %broadcast_in_dim.45, s32[64]{0:T(128)S(1)} %get-tuple-element.8, f32[64,2,4,128]{3,2,1,0:T(4,128)S(1)} %bitcast.210), kind=kCustom, calls=%fused_computation.13 | custom fusion | flops 65536 | bytes 786688 | tf_op jit(solution)/shard_map/scatter-add | solution.py:90
  41.5 3.4 %collective-permute-start = (bf16[2,4,8,128]{3,1,2,0:T(4,128)(2,1)S(1)}, bf16[2,4,8,128]{3,1,2,0:T(4,128)(2,1)S(1)}, u32[]{:S(2)}, u32[]{:S(2)}) collective-permute-start(bf16[2,4,8,128]{3,1,2,0:T(4,128)(2,1)S(1)} %get-tuple-element.23), channel_id=1, source_target_pairs={{0,1},{2,3},{4,5},{6,7},{8,9},{10,11},{12,13},{14,15},{16,17},{18,... | collective-permute-start | bytes 49160 | tf_op jit(solution)/shard_map/ppermute | solution.py:25
  44.9 1.3 %collective-permute-start.1 = (bf16[2,4,8,128]{3,1,2,0:T(4,128)(2,1)S(1)}, bf16[2,4,8,128]{3,1,2,0:T(4,128)(2,1)S(1)}, u32[]{:S(2)}, u32[]{:S(2)}) collective-permute-start(bf16[2,4,8,128]{3,1,2,0:T(4,128)(2,1)S(1)} %get-tuple-element.24), channel_id=1, source_target_pairs={{1,0},{3,2},{5,4},{7,6},{9,8},{11,10},{13,12},{15,14},{17,16},{19,... | collective-permute-start | bytes 49160 | tf_op jit(solution)/shard_map/ppermute | solution.py:27
  47.2 3.4 %collective-permute-done.1 = bf16[2,4,8,128]{3,1,2,0:T(4,128)(2,1)S(1)} collective-permute-done((bf16[2,4,8,128]{3,1,2,0:T(4,128)(2,1)S(1)}, bf16[2,4,8,128]{3,1,2,0:T(4,128)(2,1)S(1)}, u32[]{:S(2)}, u32[]{:S(2)}) %collective-permute-start.1) | collective-permute-done | bytes 16416 | tf_op jit(solution)/shard_map/ppermute | solution.py:27
  51.3 1.0 %gather_fusion.6 = bf16[256,4,128]{2,1,0:T(4,128)(2,1)S(1)} fusion(bf16[4,272,128]{2,0,1:T(4,128)(2,1)S(1)} %get-tuple-element.19, s32[1024]{0:T(1024)S(1)} %get-tuple-element.39), kind=kCustom, calls=%fused_computation.5.clone | custom fusion | bytes 525312 | tf_op jit(solution)/shard_map/jit(_take)/gather | solution.py:52
  52.2 1.0 %gather_fusion.4 = bf16[256,4,128]{2,1,0:T(4,128)(2,1)S(1)} fusion(bf16[4,272,128]{2,0,1:T(4,128)(2,1)S(1)} %get-tuple-element.19, s32[1024]{0:T(1024)S(1)} %get-tuple-element.40), kind=kCustom, calls=%fused_computation.3.clone | custom fusion | bytes 525312 | tf_op jit(solution)/shard_map/jit(_take)/gather | solution.py:52
  53.2 1.0 %gather_fusion.5 = bf16[256,4,128]{2,1,0:T(4,128)(2,1)S(1)} fusion(bf16[4,272,128]{2,0,1:T(4,128)(2,1)S(1)} %get-tuple-element.20, s32[1024]{0:T(1024)S(1)} %get-tuple-element.39), kind=kCustom, calls=%fused_computation.4.clone | custom fusion | bytes 525312 | tf_op jit(solution)/shard_map/jit(_take)/gather | solution.py:51
  54.2 1.0 %gather_fusion.3 = bf16[256,4,128]{2,1,0:T(4,128)(2,1)S(1)} fusion(bf16[4,272,128]{2,0,1:T(4,128)(2,1)S(1)} %get-tuple-element.20, s32[1024]{0:T(1024)S(1)} %get-tuple-element.40), kind=kCustom, calls=%fused_computation.2.clone | custom fusion | bytes 525312 | tf_op jit(solution)/shard_map/jit(_take)/gather | solution.py:51
  55.2 1.7 %gather_fusion.2 = bf16[256,4,128]{2,1,0:T(4,128)(2,1)} fusion(bf16[4,272,128]{2,0,1:T(4,128)(2,1)S(1)} %get-tuple-element.19, s32[1024]{0:T(1024)S(1)} %get-tuple-element.41), kind=kCustom, calls=%fused_computation.1.clone | custom fusion | bytes 525312 | tf_op jit(solution)/shard_map/jit(_take)/gather | solution.py:52
  57.9 5.3 %fusion.37 = (bf16[1,4,256,128]{3,1,2,0:T(4,128)(2,1)S(1)}, f32[4,256,128]{2,0,1:T(4,128)S(1)}, f32[4,256,128]{2,0,1:T(4,128)S(1)}) fusion(f32[4,256]{0,1:T(8,128)S(1)} %copy.24, f32[4,256]{0,1:T(8,128)S(1)} %copy.21, bf16[256,4,128]{2,1,0:T(4,128)(2,1)S(1)} %gather_fusion.5, f32[4,256]{0,1:T(8,128)S(1)} %copy.29, bf16[256,4,128]{2,1,0:T(4,128)(2,1)S(1)} %gather_fusion.6, ...), kind=kLoop, calls=%fused_computation.96 | loop fusion | flops 5505024 | bytes 3441408 | tf_op jit(solution)/shard_map/stack | solution.py:100
  63.9 1.6 %collective-permute-start.2 = (bf16[2,4,8,128]{3,1,2,0:T(4,128)(2,1)S(1)}, bf16[2,4,8,128]{3,1,2,0:T(4,128)(2,1)S(1)}, u32[]{:S(2)}, u32[]{:S(2)}) collective-permute-start(bf16[2,4,8,128]{3,1,2,0:T(4,128)(2,1)S(1)} %get-tuple-element.21), channel_id=1, source_target_pairs={{0,1},{2,3},{4,5},{6,7},{8,9},{10,11},{12,13},{14,15},{16,17},{18,... | collective-permute-start | bytes 49160 | tf_op jit(solution)/shard_map/ppermute | solution.py:25
  65.5 1.5 %collective-permute-start.3 = (bf16[2,4,8,128]{3,1,2,0:T(4,128)(2,1)S(1)}, bf16[2,4,8,128]{3,1,2,0:T(4,128)(2,1)S(1)}, u32[]{:S(2)}, u32[]{:S(2)}) collective-permute-start(bf16[2,4,8,128]{3,1,2,0:T(4,128)(2,1)S(1)} %get-tuple-element.22), channel_id=1, source_target_pairs={{1,0},{3,2},{5,4},{7,6},{9,8},{11,10},{13,12},{15,14},{17,16},{19,... | collective-permute-start | bytes 49160 | tf_op jit(solution)/shard_map/ppermute | solution.py:27
  67.0 4.1 %collective-permute-done.3 = bf16[2,4,8,128]{3,1,2,0:T(4,128)(2,1)S(1)} collective-permute-done((bf16[2,4,8,128]{3,1,2,0:T(4,128)(2,1)S(1)}, bf16[2,4,8,128]{3,1,2,0:T(4,128)(2,1)S(1)}, u32[]{:S(2)}, u32[]{:S(2)}) %collective-permute-start.3) | collective-permute-done | bytes 16416 | tf_op jit(solution)/shard_map/ppermute | solution.py:27
  71.8 1.0 %gather_fusion.12 = bf16[256,4,128]{2,1,0:T(4,128)(2,1)S(1)} fusion(bf16[4,272,128]{2,0,1:T(4,128)(2,1)S(1)} %get-tuple-element.17, s32[1024]{0:T(1024)S(1)} %get-tuple-element.39), kind=kCustom, calls=%fused_computation.11.clone | custom fusion | bytes 525312 | tf_op jit(solution)/shard_map/jit(_take)/gather | solution.py:52
  72.8 1.0 %gather_fusion.10 = bf16[256,4,128]{2,1,0:T(4,128)(2,1)S(1)} fusion(bf16[4,272,128]{2,0,1:T(4,128)(2,1)S(1)} %get-tuple-element.17, s32[1024]{0:T(1024)S(1)} %get-tuple-element.40), kind=kCustom, calls=%fused_computation.9.clone | custom fusion | bytes 525312 | tf_op jit(solution)/shard_map/jit(_take)/gather | solution.py:52
  74.8 1.0 %gather_fusion.11 = bf16[256,4,128]{2,1,0:T(4,128)(2,1)S(1)} fusion(bf16[4,272,128]{2,0,1:T(4,128)(2,1)S(1)} %get-tuple-element.18, s32[1024]{0:T(1024)S(1)} %get-tuple-element.39), kind=kCustom, calls=%fused_computation.10.clone | custom fusion | bytes 525312 | tf_op jit(solution)/shard_map/jit(_take)/gather | solution.py:51
  76.8 1.1 %gather_fusion.9 = bf16[256,4,128]{2,1,0:T(4,128)(2,1)S(1)} fusion(bf16[4,272,128]{2,0,1:T(4,128)(2,1)S(1)} %get-tuple-element.18, s32[1024]{0:T(1024)} %copy-done.2), kind=kCustom, calls=%fused_computation.8.clone | custom fusion | bytes 525312 | tf_op jit(solution)/shard_map/jit(_take)/gather | solution.py:51
  77.9 4.5 %fusion.39 = (bf16[1,4,256,128]{3,1,2,0:T(4,128)(2,1)S(1)}, f32[4,256,128]{2,0,1:T(4,128)S(1)}, f32[4,256,128]{2,0,1:T(4,128)S(1)}) fusion(f32[4,256]{0,1:T(8,128)S(1)} %copy.24, f32[4,256]{0,1:T(8,128)S(1)} %copy.21, bf16[256,4,128]{2,1,0:T(4,128)(2,1)S(1)} %gather_fusion.11, f32[4,256]{0,1:T(8,128)S(1)} %copy.29, ...), kind=kLoop, calls=%fused_computation.98 | loop fusion | flops 5505024 | bytes 3441408 | tf_op jit(solution)/shard_map/stack | solution.py:111
  85.1 3.5 %all-to-all-start.1 = ((bf16[2,4,64,128]{3,1,0,2:T(4,128)(2,1)}), bf16[2,4,64,128]{3,1,0,2:T(4,128)(2,1)S(1)}, u32[]{:S(2)}, u32[]{:S(2)}) async-start(bf16[2,4,64,128]{3,1,0,2:T(4,128)(2,1)} %select_bitcast_fusion), calls=%async_computation.1 | async-start | bytes 262144 | tf_op jit(solution)/shard_map/all_to_all | solution.py:113
  89.5 7.0 %all-to-all-done.1 = bf16[2,4,64,128]{3,1,0,2:T(4,128)(2,1)S(1)} async-done(((bf16[2,4,64,128]{3,1,0,2:T(4,128)(2,1)}), bf16[2,4,64,128]{3,1,0,2:T(4,128)(2,1)S(1)}, u32[]{:S(2)}, u32[]{:S(2)}) %all-to-all-start.1) | async-done | bytes 131104 | tf_op jit(solution)/shard_map/all_to_all | solution.py:113
  (84 shorter events, 23.9 us)
Async XLA Ops:
  0.6 2.1 %copy-start = (bf16[2,64,4,128]{3,2,1,0:T(4,128)(2,1)S(1)}, bf16[2,64,4,128]{3,2,1,0:T(4,128)(2,1)}, u32[]{:S(2)}) copy-start(bf16[2,64,4,128]{3,2,1,0:T(4,128)(2,1)} %param.9) | copy-start | bytes 393220
  2.8 18.6 %copy-start.5 = (s32[3,256]{1,0:T(4,128)S(1)}, s32[3,256]{1,0:T(4,128)}, u32[]{:S(2)}) copy-start(s32[3,256]{1,0:T(4,128)} %param.15) | copy-start | bytes 9220
  2.8 18.7 %copy-start.9 = (u32[32]{0:T(128)S(1)}, u32[32]{0:T(128)}, u32[]{:S(2)}) copy-start(u32[32]{0:T(128)} %constant.65) | copy-start | bytes 388
  2.8 19.9 %copy-start.8 = (s32[4]{0:T(128)S(1)}, s32[4]{0:T(128)}, u32[]{:S(2)}) copy-start(s32[4]{0:T(128)} %param.13) | copy-start | bytes 52
  2.8 32.6 %copy-start.1 = (f32[2,4,4,256]{3,2,1,0:T(4,128)S(1)}, f32[2,4,4,256]{3,2,1,0:T(4,128)}, u32[]{:S(2)}) copy-start(f32[2,4,4,256]{3,2,1,0:T(4,128)} %param.14) | copy-start | bytes 98308
  14.0 22.9 %all-to-all-start = ((bf16[16,2,4,4,128]{4,2,1,3,0:T(4,128)(2,1)}), bf16[16,2,4,4,128]{4,2,1,3,0:T(4,128)(2,1)S(1)}, u32[]{:S(2)}, u32[]{:S(2)}) async-start(bf16[16,2,4,4,128]{4,2,1,3,0:T(4,128)(2,1)} %constant_dynamic-update-slice_fusion), calls=%async_computation | async-start | bytes 262144 | tf_op jit(solution)/shard_map/all_to_all | solution.py:83
  21.4 36.4 %copy-start.7 = (pred[256]{0:T(512)(128)(4,1)}, pred[256]{0:T(512)(128)(4,1)S(1)}, u32[]{:S(2)}) copy-start(pred[256]{0:T(512)(128)(4,1)S(1)} %compare_and_fusion.2) | copy-start | bytes 772
  36.8 21.1 %copy-start.3 = (pred[256]{0:T(512)(128)(4,1)}, pred[256]{0:T(512)(128)(4,1)S(1)}, u32[]{:S(2)}) copy-start(pred[256]{0:T(512)(128)(4,1)S(1)} %get-tuple-element.42) | copy-start | bytes 772
  36.8 21.1 %copy-start.4 = (pred[256]{0:T(512)(128)(4,1)}, pred[256]{0:T(512)(128)(4,1)S(1)}, u32[]{:S(2)}) copy-start(pred[256]{0:T(512)(128)(4,1)S(1)} %get-tuple-element.43) | copy-start | bytes 772
  41.5 5.7 %collective-permute-start = (bf16[2,4,8,128]{3,1,2,0:T(4,128)(2,1)S(1)}, bf16[2,4,8,128]{3,1,2,0:T(4,128)(2,1)S(1)}, u32[]{:S(2)}, u32[]{:S(2)}) collective-permute-start(bf16[2,4,8,128]{3,1,2,0:T(4,128)(2,1)S(1)} %get-tuple-element.23), channel_id=1, source_target_pairs={{0,1},{2,3},{4,5},{6,7},{8,9},{10,11},{12,13},{14,15},{16,17},{18,... | collective-permute-start | bytes 49160 | tf_op jit(solution)/shard_map/ppermute | solution.py:25
  44.9 5.6 %collective-permute-start.1 = (bf16[2,4,8,128]{3,1,2,0:T(4,128)(2,1)S(1)}, bf16[2,4,8,128]{3,1,2,0:T(4,128)(2,1)S(1)}, u32[]{:S(2)}, u32[]{:S(2)}) collective-permute-start(bf16[2,4,8,128]{3,1,2,0:T(4,128)(2,1)S(1)} %get-tuple-element.24), channel_id=1, source_target_pairs={{1,0},{3,2},{5,4},{7,6},{9,8},{11,10},{13,12},{15,14},{17,16},{19,... | collective-permute-start | bytes 49160 | tf_op jit(solution)/shard_map/ppermute | solution.py:27
  46.3 26.6 %copy-start.2 = (s32[1024]{0:T(1024)}, s32[1024]{0:T(1024)S(1)}, u32[]{:S(2)}) copy-start(s32[1024]{0:T(1024)S(1)} %get-tuple-element.40) | copy-start | bytes 12292
  63.9 3.1 %collective-permute-start.2 = (bf16[2,4,8,128]{3,1,2,0:T(4,128)(2,1)S(1)}, bf16[2,4,8,128]{3,1,2,0:T(4,128)(2,1)S(1)}, u32[]{:S(2)}, u32[]{:S(2)}) collective-permute-start(bf16[2,4,8,128]{3,1,2,0:T(4,128)(2,1)S(1)} %get-tuple-element.21), channel_id=1, source_target_pairs={{0,1},{2,3},{4,5},{6,7},{8,9},{10,11},{12,13},{14,15},{16,17},{18,... | collective-permute-start | bytes 49160 | tf_op jit(solution)/shard_map/ppermute | solution.py:25
  65.5 5.6 %collective-permute-start.3 = (bf16[2,4,8,128]{3,1,2,0:T(4,128)(2,1)S(1)}, bf16[2,4,8,128]{3,1,2,0:T(4,128)(2,1)S(1)}, u32[]{:S(2)}, u32[]{:S(2)}) collective-permute-start(bf16[2,4,8,128]{3,1,2,0:T(4,128)(2,1)S(1)} %get-tuple-element.22), channel_id=1, source_target_pairs={{1,0},{3,2},{5,4},{7,6},{9,8},{11,10},{13,12},{15,14},{17,16},{19,... | collective-permute-start | bytes 49160 | tf_op jit(solution)/shard_map/ppermute | solution.py:27
  83.0 1.2 %copy-start.6 = (pred[64]{0:T(512)(128)(4,1)S(1)}, pred[64]{0:T(512)(128)(4,1)}, u32[]{:S(2)}) copy-start(pred[64]{0:T(512)(128)(4,1)} %get-tuple-element.7) | copy-start | bytes 196
  85.1 11.4 %all-to-all-start.1 = ((bf16[2,4,64,128]{3,1,0,2:T(4,128)(2,1)}), bf16[2,4,64,128]{3,1,0,2:T(4,128)(2,1)S(1)}, u32[]{:S(2)}, u32[]{:S(2)}) async-start(bf16[2,4,64,128]{3,1,0,2:T(4,128)(2,1)} %select_bitcast_fusion), calls=%async_computation.1 | async-start | bytes 262144 | tf_op jit(solution)/shard_map/all_to_all | solution.py:113
